TPU v7x, 32 devices: a whole 2x2x4 slice. The times are simulated.
32 devices in a mesh: groups: 2 (over x), tm: 16 (over z, y, core).
Axes of the slice: x: 2, y: 2, z: 4, core: 2. Of those that a mesh axis runs over, the one named last changes fastest.
Arguments:
- queries: bfloat16 [6144, 2560], P(('groups', 'tm')), parts along dimension 0, may hold values from -6 to 6
- keys: bfloat16 [6144, 2560], P(('groups', 'tm')), parts along dimension 0, may hold values from -6 to 6
- values: bfloat16 [6144, 2560], P(('groups', 'tm')), parts along dimension 0, may hold values from -6 to 6
- q_gain: float32 [2560], replicated, may hold values from 0.5 to 1.5
- k_gain: float32 [2560], replicated, may hold values from 0.5 to 1.5
- out_weight: bfloat16 [2560, 5120], P('tm'), may hold values from -0.125 to 0.125
- out_gate: float32 [5120], replicated, may hold values from 0.5 to 2
- reach: int32 [32, 2], P(('groups', 'tm')), parts along dimension 0, may hold values from 0 to 1
Outputs:
- mixed: bfloat16 [6144, 5120], P(('groups', 'tm')), parts along dimension 0
There are 2 independent parts, one for each index of `groups`. A program takes and returns all parts, laid end to end along the dimension named above; an argument that names none is the same for every part. Nothing has to cross between parts.
Inputs may be any that keep to these rules, and one draw needn't show every extreme that they name: `reach`: requests past the first or last tile are ignored.
All inputs are finite; a program needn't handle non-finite values.
Results may differ from a plain program's by a relative error of at most 0.0076.
Values may be sent and summed in bfloat16 or wider, within the bound.
A program may use at most 128 MiB of HBM per device.

v0:
```python
import jax
import jax.numpy as jnp
from jax import lax
from jax.sharding import PartitionSpec as P

HD = 128
TT = 4
TH = 6
TW = 8


def shifted(shard, axis, by):
    peers = lax.axis_size(axis)
    pairs = [(i, i + by) for i in range(peers) if 0 <= i + by < peers]
    return lax.ppermute(shard, axis, pairs)


def rms_scaled(block, gain):
    values32 = block.astype(jnp.float32)
    inverse = lax.rsqrt(jnp.mean(values32 * values32, axis=-1, keepdims=True) + 1e-06)
    return (values32 * inverse * gain).astype(jnp.bfloat16)


def local(queries, keys, values, q_gain, k_gain, out_weight, out_gate, reach):
    tile = TT * TH * TW
    rows = queries.shape[0]
    chans = queries.shape[1]
    heads = chans // HD
    count = rows // tile
    scale = HD ** (-0.5)
    q_norm = rms_scaled(queries, q_gain)
    k_norm = rms_scaled(keys, k_gain)
    before_k, before_v = shifted((k_norm, values), "tm", 1)
    after_k, after_v = shifted((k_norm, values), "tm", -1)
    key_buffer = jnp.concatenate([before_k, k_norm, after_k], axis=0).reshape(
        count + 2, tile, heads, HD
    )
    val_buffer = jnp.concatenate([before_v, values, after_v], axis=0).reshape(
        count + 2, tile, heads, HD
    )
    position = lax.axis_index("tm")
    first_tile = position * count
    total_tiles = lax.axis_size("tm") * count
    global_tile = first_tile + jnp.arange(count, dtype=jnp.int32)
    valid = jnp.stack(
        [
            (reach[:, 0] == 1) & (global_tile > 0),
            global_tile >= 0,
            (reach[:, 1] == 1) & (global_tile < total_tiles - 1),
        ],
        axis=1,
    )
    query_tiles = q_norm.reshape(count, tile, heads, HD)
    seen_k = jnp.stack([key_buffer[offset : offset + count] for offset in range(3)], axis=1)
    seen_v = jnp.stack([val_buffer[offset : offset + count] for offset in range(3)], axis=1)
    logits = (
        jnp.einsum("nqhd,nokhd->nhqok", query_tiles, seen_k, preferred_element_type=jnp.float32)
        * scale
    )
    logits = jnp.where(valid[:, None, None, :, None], logits, -1e30)
    logits = logits.reshape(count, heads, tile, 3 * tile)
    top = jnp.max(logits, axis=-1, keepdims=True)
    expo = jnp.exp(logits - top)
    weights = (expo / jnp.sum(expo, axis=-1, keepdims=True)).astype(jnp.bfloat16)
    attended = jnp.einsum(
        "nhqk,nkhd->nqhd",
        weights,
        seen_v.reshape(count, 3 * tile, heads, HD),
        preferred_element_type=jnp.float32,
    ).astype(jnp.bfloat16)
    attended = attended.reshape(rows, chans)
    full_weight = lax.all_gather(out_weight, "tm", axis=0, tiled=True)
    projected = jnp.dot(attended, full_weight, preferred_element_type=jnp.float32)
    return (out_gate * projected).astype(jnp.bfloat16)


def solution(mesh):
    return jax.shard_map(
        local,
        mesh=mesh,
        in_specs=(
            P(("groups", "tm"), None),
            P(("groups", "tm"), None),
            P(("groups", "tm"), None),
            P(),
            P(),
            P("tm", None),
            P(),
            P(("groups", "tm"), None),
        ),
        out_specs=P(("groups", "tm"), None),
        check_vma=False,
    )
```

profile of v0, /device:TPU:27, one launch (start us, length us, event | category | flops | bytes accessed | tf_op | source)
XLA Modules:
  0.0 202.7 jit_solution(11805782908131688679)
XLA Ops:
  6.5 0.0 copy-start.1
  6.5 0.0 all-gather.2.cloned.1.call-start
  6.5 0.7 all-gather.2.cloned.1.call-update
  7.3 1.5 fusion.5
  8.7 0.0 copy-done.1
  8.8 0.0 copy-start.6
  8.8 1.0 fusion.7
  9.8 3.7 %collective-permute-start.2 = (bf16[192,2560]{1,0:T(8,128)(2,1)S(1)}, bf16[192,2560]{1,0:T(8,128)(2,1)}, u32[]{:S(2)}, u32[]{:S(2)}) collective-permute-start(bf16[192,2560]{1,0:T(8,128)(2,1)S(1)} %fusion.7), channel_id=1, source_target_pairs={{0,1},{1,2},{2,3},{3,4},{4,5},{5,6},{6,7},{7,8},{8,9},{9,10},{10,1... | collective-permute-start | bytes 2949128 | tf_op jit(solution)/shard_map/ppermute | solution.py:15
  13.5 1.9 collective-permute-start.3
  15.4 3.6 %collective-permute-start = (bf16[192,2560]{1,0:T(8,128)(2,1)}, bf16[192,2560]{1,0:T(8,128)(2,1)}, u32[]{:S(2)}, u32[]{:S(2)}) collective-permute-start(bf16[192,2560]{1,0:T(8,128)(2,1)} %param.10), channel_id=1, source_target_pairs={{0,1},{1,2},{2,3},{3,4},{4,5},{5,6},{6,7},{7,8},{8,9},{9,10},{10,1... | collective-permute-start | bytes 2949128 | tf_op jit(solution)/shard_map/ppermute | solution.py:15
  19.1 1.9 collective-permute-start.1
  21.0 0.7 stack.45
  21.7 1.7 stack.37
  23.3 0.0 copy-done.6
  23.4 0.6 fusion.17
  25.3 1.2 copy.16
  26.5 0.1 add_bitcast_fusion
  26.5 1.5 fusion.2
  28.0 11.8 %collective-permute-done.2 = bf16[192,2560]{1,0:T(8,128)(2,1)} collective-permute-done((bf16[192,2560]{1,0:T(8,128)(2,1)S(1)}, bf16[192,2560]{1,0:T(8,128)(2,1)}, u32[]{:S(2)}, u32[]{:S(2)}) %collective-permute-start.2) | collective-permute-done | bytes 983072 | tf_op jit(solution)/shard_map/ppermute | solution.py:15
  39.9 1.7 stack.44
  41.5 1.2 copy.15
  42.7 0.0 copy-start.3
  42.7 23.5 %collective-permute-done.3 = bf16[192,2560]{1,0:T(8,128)(2,1)} collective-permute-done((bf16[192,2560]{1,0:T(8,128)(2,1)S(1)}, bf16[192,2560]{1,0:T(8,128)(2,1)}, u32[]{:S(2)}, u32[]{:S(2)}) %collective-permute-start.3) | collective-permute-done | bytes 983072 | tf_op jit(solution)/shard_map/ppermute | solution.py:15
  66.2 1.7 stack.46
  67.8 0.2 copy.17
  68.0 0.0 copy-done.3
  68.0 0.0 copy-start.2
  68.1 0.0 copy-start.5
  68.1 1.6 pad_maximum_fusion.1
  69.7 0.0 copy-done.2
  69.7 0.0 copy-done.5
  69.7 6.1 %fusion.13 = f32[20,192,576]{1,2,0} fusion(bf16[20,128,576]{1,2,0:T(8,128)(2,1)S(1)} %bitcast.38, bf16[192,2560]{1,0:T(8,128)(2,1)S(1)} %copy-done.2, f32[2560]{0:T(1024)S(1)} %copy-done.5, f32[192]{0:T(256)S(1)} %add_rsqrt_fusion.1), kind=kOutput, calls=%fused_computation.23 | convolution fusion | flops 568197120 | bytes 12790528
  75.8 12.3 %fusion.16 = (f32[20,192]{1,0:T(8,128)}, f32[20,192,3,192]{1,3,2,0:T(8,128)}) fusion(f32[20,192,3,192]{1,3,2,0:T(8,128)} %bitcast.37, pred[3]{0:T(512)(128)(4,1)S(1)} %add_bitcast_fusion), kind=kLoop, calls=%fused_computation.29 | loop fusion | flops 6631680 | bytes 17710084 | tf_op jit(solution)/shard_map/reduce_max | solution.py:62
  88.1 11.7 %copy.19 = f32[20,192,576]{2,1,0:T(8,128)} copy(f32[20,192,576]{1,2,0:T(8,128)} %bitcast.36) | data formatting | bytes 17694720 | tf_op jit(solution)/shard_map/reshape | solution.py:61
  99.8 0.0 collective-permute-done
  99.8 1.7 stack.36
  101.5 0.0 collective-permute-done.1
  101.5 1.7 stack.38
  103.2 0.0 copy-start
  103.2 0.6 pad_maximum_fusion
  103.9 0.0 copy-start.4
  103.9 0.7 copy.14
  104.6 3.1 %copy-done = f32[20,192,3,192]{1,3,2,0:T(8,128)S(1)} copy-done((f32[20,192,3,192]{1,3,2,0:T(8,128)S(1)}, f32[20,192,3,192]{1,3,2,0:T(8,128)}, u32[]{:S(2)}) %copy-start) | copy-done | bytes 8847384
  107.7 0.0 copy-done.4
  107.7 1.8 exponential_reduce_fusion
  109.5 0.0 copy-start.7
  109.5 5.4 %fusion.9 = bf16[1,192,20,128]{3,1,2,0:T(8,128)(2,1)S(1)} fusion(bf16[576,20,128]{2,0,1:T(8,128)(2,1)S(1)} %bitcast.39, f32[20,192,576]{2,1,0:T(8,128)} %copy.19, f32[20,192]{1,0:T(8,128)S(1)} %exponential_reduce_fusion, f32[20,192]{1,0:T(8,128)S(1)} %copy-done.4), kind=kOutput, calls=%fused_computation.19 | convolution fusion | flops 573358080 | bytes 12810240 | tf_op jit(solution)/shard_map/nhqk,nkhd->nqhd/dot_general | solution.py:65
  114.9 0.7 copy.20
  115.6 67.5 %all-gather.2.cloned.1.call-done = bf16[2560,5120]{1,0:T(8,128)(2,1)} async-done(((bf16[160,5120]{1,0:T(8,128)(2,1)}), bf16[2560,5120]{1,0:T(8,128)(2,1)}) %all-gather.2.cloned.1.call-update) | async-done | bytes 26214416 | tf_op jit(solution)/shard_map/all_gather | solution.py:72
  183.1 0.0 copy-done.7
  183.1 12.7 %fusion = bf16[192,5120]{1,0:T(8,128)(2,1)} fusion(bf16[2560,5120]{1,0:T(8,128)(2,1)} %all-gather.2.cloned.1.call-done, f32[5120]{0:T(1024)S(1)} %copy-done.7, bf16[24,8,20,128]{3,2,1,0:T(8,128)(2,1)S(1)} %bitcast.40), kind=kOutput, calls=%fused_computation.4 | convolution fusion | flops 5035130880 | bytes 29184000 | tf_op jit(solution)/shard_map/dot_general | solution.py:73
  (2 shorter events, 0.0 us)
Async XLA Ops:
  6.5 2.2 %copy-start.1 = (bf16[192,2560]{1,0:T(8,128)(2,1)S(1)}, bf16[192,2560]{1,0:T(8,128)(2,1)}, u32[]{:S(2)}) copy-start(bf16[192,2560]{1,0:T(8,128)(2,1)} %param.9) | copy-start | bytes 2949124
  6.5 176.5 %all-gather.2.cloned.1.call-start = ((), (), s32[]{:S(2)}) async-start(), calls=%async_computation | async-start | bytes 27852800 | tf_op jit(solution)/shard_map/all_gather | solution.py:72
  8.8 14.6 %copy-start.6 = (s32[1,2]{1,0:T(1,128)S(1)}, s32[1,2]{1,0:T(1,128)}, u32[]{:S(2)}) copy-start(s32[1,2]{1,0:T(1,128)} %param.15) | copy-start | bytes 28
  9.8 30.1 %collective-permute-start.2 = (bf16[192,2560]{1,0:T(8,128)(2,1)S(1)}, bf16[192,2560]{1,0:T(8,128)(2,1)}, u32[]{:S(2)}, u32[]{:S(2)}) collective-permute-start(bf16[192,2560]{1,0:T(8,128)(2,1)S(1)} %fusion.7), channel_id=1, source_target_pairs={{0,1},{1,2},{2,3},{3,4},{4,5},{5,6},{6,7},{7,8},{8,9},{9,10},{10,1... | collective-permute-start | bytes 2949128 | tf_op jit(solution)/shard_map/ppermute | solution.py:15
  13.5 52.7 %collective-permute-start.3 = (bf16[192,2560]{1,0:T(8,128)(2,1)S(1)}, bf16[192,2560]{1,0:T(8,128)(2,1)}, u32[]{:S(2)}, u32[]{:S(2)}) collective-permute-start(bf16[192,2560]{1,0:T(8,128)(2,1)S(1)} %fusion.7), channel_id=1, source_target_pairs={{1,0},{2,1},{3,2},{4,3},{5,4},{6,5},{7,6},{8,7},{9,8},{10,9},{11,1... | collective-permute-start | bytes 2949128 | tf_op jit(solution)/shard_map/ppermute | solution.py:15
  15.4 84.4 %collective-permute-start = (bf16[192,2560]{1,0:T(8,128)(2,1)}, bf16[192,2560]{1,0:T(8,128)(2,1)}, u32[]{:S(2)}, u32[]{:S(2)}) collective-permute-start(bf16[192,2560]{1,0:T(8,128)(2,1)} %param.10), channel_id=1, source_target_pairs={{0,1},{1,2},{2,3},{3,4},{4,5},{5,6},{6,7},{7,8},{8,9},{9,10},{10,1... | collective-permute-start | bytes 2949128 | tf_op jit(solution)/shard_map/ppermute | solution.py:15
  19.1 82.4 %collective-permute-start.1 = (bf16[192,2560]{1,0:T(8,128)(2,1)}, bf16[192,2560]{1,0:T(8,128)(2,1)}, u32[]{:S(2)}, u32[]{:S(2)}) collective-permute-start(bf16[192,2560]{1,0:T(8,128)(2,1)} %param.10), channel_id=1, source_target_pairs={{1,0},{2,1},{3,2},{4,3},{5,4},{6,5},{7,6},{8,7},{9,8},{10,9},{11,1... | collective-permute-start | bytes 2949128 | tf_op jit(solution)/shard_map/ppermute | solution.py:15
  42.7 25.3 %copy-start.3 = (bf16[1,1,192,20,128]{4,2,1,3,0:T(8,128)(2,1)S(1)}, bf16[1,1,192,20,128]{4,2,1,3,0:T(8,128)(2,1)}, u32[]{:S(2)}) copy-start(bf16[1,1,192,20,128]{4,2,1,3,0:T(8,128)(2,1)} %copy.16) | copy-start | bytes 2949124
  68.0 1.7 copy-start.2
  68.1 1.7 copy-start.5
  103.2 4.5 %copy-start = (f32[20,192,3,192]{1,3,2,0:T(8,128)S(1)}, f32[20,192,3,192]{1,3,2,0:T(8,128)}, u32[]{:S(2)}) copy-start(f32[20,192,3,192]{1,3,2,0:T(8,128)} %get-tuple-element.6) | copy-start | bytes 26542084
  103.9 3.9 %copy-start.4 = (f32[20,192]{1,0:T(8,128)S(1)}, f32[20,192]{1,0:T(8,128)}, u32[]{:S(2)}) copy-start(f32[20,192]{1,0:T(8,128)} %get-tuple-element.5) | copy-start | bytes 46084
  109.5 73.6 %copy-start.7 = (f32[5120]{0:T(1024)S(1)}, f32[5120]{0:T(1024)}, u32[]{:S(2)}) copy-start(f32[5120]{0:T(1024)} %param.14) | copy-start | bytes 61444
Sparse Core Ops, SparseCore 0:
  8.9 174.0 all-gather.1
where the time goes:
time: 203 us
  waiting for transfers between devices  103 us (51%)
  local copies, waits for them, and re-layouts  28.4 us (14%)
  matrix products  24.2 us (12%)
  other arithmetic  20.4 us (10%)
  between operations  14.9 us (7%)
  starting transfers between devices  11.2 us (6%)
    all_gather x1, waiting for transfers between devices, local(): full_weight = lax.all_gather(out_weight, 'tm', axis=0, tiled=True)  67.5 us
    ppermute x4, waiting for transfers between devices, shifted(): return lax.ppermute(shard, axis, pairs)  35.3 us
    dot_general x1, matrix products, local(): jnp.dot(attended, full_weight, preferred_element_type=jnp.float32)  12.7 us
    reduce_max x1, other arithmetic, local(): top = jnp.max(logits, axis=-1, keepdims=True)  12.3 us
    reshape x1, local copies, waits for them, and re-layouts, local(): logits = logits.reshape(count, heads, tile, 3 * tile)  11.7 us
    ppermute x4, starting transfers between devices, shifted(): return lax.ppermute(shard, axis, pairs)  11.2 us
    another operation x6, local copies, waits for them, and re-layouts, local(): jnp.stack([key_buffer[offset:offset + count] for offset in range(3)], axi...  6.51 us
    unnamed x1, matrix products  6.05 us
  transfers between devices with their start and end apart: 5, of which 3 were waited for; matrix products, arithmetic and copies ran while one was open for 28% of the time, Pallas kernels for 0%

commit v1 on v0

--- a/solution.py
+++ b/solution.py
@@ -69,7 +69,8 @@
         preferred_element_type=jnp.float32,
     ).astype(jnp.bfloat16)
     attended = attended.reshape(rows, chans)
-    full_weight = lax.all_gather(out_weight, "tm", axis=0, tiled=True)
+    sent = jnp.stack([out_weight] * lax.axis_size("tm"))
+    full_weight = jnp.concatenate(lax.all_to_all(sent, "tm", 0, 0), axis=0)
     projected = jnp.dot(attended, full_weight, preferred_element_type=jnp.float32)
     return (out_gate * projected).astype(jnp.bfloat16)
 

time: 203 us -> 661 us (3.26)
  the two profiles are of different devices: /device:TPU:27 before, /device:TPU:15 now
where the time goes in v1:
time: 661 us; the launch traced here: 660 us
  waiting for transfers between devices  558 us (84%)
  local copies, waits for them, and re-layouts  38.5 us (6%)
  matrix products  22.1 us (3%)
  other arithmetic  20.5 us (3%)
  starting transfers between devices  19.7 us (3%)
    ppermute x4, waiting for transfers between devices, shifted(): return lax.ppermute(shard, axis, pairs)  558 us
  transfers between devices with their start and end apart: 5, of which 2 were waited for; matrix products, arithmetic and copies ran while one was open for 9% of the time, Pallas kernels for 0%

profile of v1, /device:TPU:15, one launch (start us, length us, event | category | flops | bytes accessed | tf_op | source)
XLA Modules:
  0.0 660.0 jit_solution(12213975472313583493)
XLA Ops:
  0.0 9.7 %stack.67 = bf16[16,160,5120]{2,1,0:T(8,128)(2,1)} broadcast(bf16[160,5120]{1,0:T(8,128)(2,1)} %param.13), dimensions={1,2} | broadcast | bytes 27852800 | tf_op jit(solution)/shard_map/stack | solution.py:72
  9.7 0.0 copy-start.1
  9.7 0.0 copy-start.6
  9.7 6.7 %all-to-all-start = ((bf16[16,160,5120]{2,1,0:T(8,128)(2,1)}), bf16[16,160,5120]{2,1,0:T(8,128)(2,1)}, u32[]{:S(2)}, u32[]{:S(2)}) async-start(bf16[16,160,5120]{2,1,0:T(8,128)(2,1)} %stack.67), calls=%async_computation | async-start | bytes 52428800 | tf_op jit(solution)/shard_map/all_to_all | solution.py:73
  16.4 2.3 collective-permute-start.1
  18.7 4.2 collective-permute-start
  22.8 0.0 copy-done.1
  22.8 0.3 fusion.5
  23.1 0.0 copy-done.6
  23.1 1.2 fusion.7
  24.4 0.0 copy-start.8
  24.4 0.0 copy-start.2
  24.4 2.0 collective-permute-start.3
  26.4 4.5 collective-permute-start.2
  31.0 1.7 stack.27
  32.6 1.7 stack.64
  34.3 1.2 copy.16
  35.5 0.0 copy-done.8
  35.5 0.6 fusion.17
  37.3 0.1 add_bitcast_fusion
  37.4 0.0 copy-done.2
  37.4 0.3 fusion.2
  37.7 553.6 %collective-permute-done.1 = bf16[192,2560]{1,0:T(8,128)(2,1)} collective-permute-done((bf16[192,2560]{1,0:T(8,128)(2,1)}, bf16[192,2560]{1,0:T(8,128)(2,1)}, u32[]{:S(2)}, u32[]{:S(2)}) %collective-permute-start.1) | collective-permute-done | bytes 983072 | tf_op jit(solution)/shard_map/ppermute | solution.py:15
  591.2 1.7 stack.28
  592.9 0.0 collective-permute-done
  592.9 1.7 stack.26
  594.6 0.6 pad_maximum_fusion
  595.2 2.4 copy.14
  597.6 4.2 collective-permute-done.3
  601.8 1.7 stack.65
  603.4 0.0 copy-start.4
  603.5 0.2 copy.17
  603.7 0.0 collective-permute-done.2
  603.7 1.7 stack.63
  605.4 0.2 copy.15
  605.6 0.0 copy-done.4
  605.6 0.0 copy-start.3
  605.6 0.0 copy-start.7
  605.6 0.3 pad_maximum_fusion.1
  606.0 0.9 copy-done.3
  606.8 0.0 copy-done.7
  606.8 6.1 fusion.13
  612.9 11.4 %fusion.16 = (f32[20,192]{1,0:T(8,128)S(1)}, f32[20,192,3,192]{1,3,2,0:T(8,128)}) fusion(f32[20,192,3,192]{1,3,2,0:T(8,128)} %bitcast.38, pred[3]{0:T(512)(128)(4,1)S(1)} %add_bitcast_fusion), kind=kLoop, calls=%fused_computation.29 | loop fusion | flops 6631680 | bytes 17710084 | tf_op jit(solution)/shard_map/reduce_max | solution.py:62
  624.3 0.0 copy-start.5
  624.3 11.8 %copy.19 = f32[20,192,576]{2,1,0:T(8,128)} copy(f32[20,192,576]{1,2,0:T(8,128)} %bitcast.37) | data formatting | bytes 17694720 | tf_op jit(solution)/shard_map/reshape | solution.py:61
  636.1 0.0 copy-start
  636.1 6.3 exponential_reduce_fusion
  642.4 0.0 copy-done.5
  642.4 0.9 copy-done
  643.2 0.0 copy-start.9
  643.2 3.1 fusion.9
  646.3 0.7 copy.20
  647.0 0.0 all-to-all-done
  647.0 0.0 copy-done.9
  647.0 12.9 %fusion = bf16[192,5120]{1,0:T(8,128)(2,1)} fusion(bf16[2560,5120]{1,0:T(8,128)(2,1)} %bitcast.16, f32[5120]{0:T(1024)S(1)} %copy-done.9, bf16[24,8,20,128]{3,2,1,0:T(8,128)(2,1)S(1)} %bitcast.41), kind=kOutput, calls=%fused_computation.4 | convolution fusion | flops 5035130880 | bytes 29184000 | tf_op jit(solution)/shard_map/dot_general | solution.py:74
  (2 shorter events, 0.0 us)
Async XLA Ops:
  9.7 13.1 %copy-start.1 = (bf16[192,2560]{1,0:T(8,128)(2,1)S(1)}, bf16[192,2560]{1,0:T(8,128)(2,1)}, u32[]{:S(2)}) copy-start(bf16[192,2560]{1,0:T(8,128)(2,1)} %param.9) | copy-start | bytes 2949124
  9.7 13.4 %copy-start.6 = (f32[2560]{0:T(1024)S(1)}, f32[2560]{0:T(1024)}, u32[]{:S(2)}) copy-start(f32[2560]{0:T(1024)} %param.12) | copy-start | bytes 30724
  9.7 637.3 %all-to-all-start = ((bf16[16,160,5120]{2,1,0:T(8,128)(2,1)}), bf16[16,160,5120]{2,1,0:T(8,128)(2,1)}, u32[]{:S(2)}, u32[]{:S(2)}) async-start(bf16[16,160,5120]{2,1,0:T(8,128)(2,1)} %stack.67), calls=%async_computation | async-start | bytes 52428800 | tf_op jit(solution)/shard_map/all_to_all | solution.py:73
  16.4 574.9 %collective-permute-start.1 = (bf16[192,2560]{1,0:T(8,128)(2,1)}, bf16[192,2560]{1,0:T(8,128)(2,1)}, u32[]{:S(2)}, u32[]{:S(2)}) collective-permute-start(bf16[192,2560]{1,0:T(8,128)(2,1)} %param.10), channel_id=1, source_target_pairs={{1,0},{2,1},{3,2},{4,3},{5,4},{6,5},{7,6},{8,7},{9,8},{10,9},{11,1... | collective-permute-start | bytes 2949128 | tf_op jit(solution)/shard_map/ppermute | solution.py:15
  18.7 574.3 %collective-permute-start = (bf16[192,2560]{1,0:T(8,128)(2,1)}, bf16[192,2560]{1,0:T(8,128)(2,1)}, u32[]{:S(2)}, u32[]{:S(2)}) collective-permute-start(bf16[192,2560]{1,0:T(8,128)(2,1)} %param.10), channel_id=1, source_target_pairs={{0,1},{1,2},{2,3},{3,4},{4,5},{5,6},{6,7},{7,8},{8,9},{9,10},{10,1... | collective-permute-start | bytes 2949128 | tf_op jit(solution)/shard_map/ppermute | solution.py:15
  24.4 11.2 %copy-start.8 = (s32[1,2]{1,0:T(1,128)S(1)}, s32[1,2]{1,0:T(1,128)}, u32[]{:S(2)}) copy-start(s32[1,2]{1,0:T(1,128)} %param.15) | copy-start | bytes 28
  24.4 13.0 %copy-start.2 = (bf16[192,2560]{1,0:T(8,128)(2,1)S(1)}, bf16[192,2560]{1,0:T(8,128)(2,1)}, u32[]{:S(2)}) copy-start(bf16[192,2560]{1,0:T(8,128)(2,1)} %param.8) | copy-start | bytes 2949124
  24.4 577.4 %collective-permute-start.3 = (bf16[192,2560]{1,0:T(8,128)(2,1)}, bf16[192,2560]{1,0:T(8,128)(2,1)}, u32[]{:S(2)}, u32[]{:S(2)}) collective-permute-start(bf16[192,2560]{1,0:T(8,128)(2,1)} %fusion.7), channel_id=1, source_target_pairs={{1,0},{2,1},{3,2},{4,3},{5,4},{6,5},{7,6},{8,7},{9,8},{10,9},{11,1... | collective-permute-start | bytes 2949128 | tf_op jit(solution)/shard_map/ppermute | solution.py:15
  26.4 577.2 %collective-permute-start.2 = (bf16[192,2560]{1,0:T(8,128)(2,1)}, bf16[192,2560]{1,0:T(8,128)(2,1)}, u32[]{:S(2)}, u32[]{:S(2)}) collective-permute-start(bf16[192,2560]{1,0:T(8,128)(2,1)} %fusion.7), channel_id=1, source_target_pairs={{0,1},{1,2},{2,3},{3,4},{4,5},{5,6},{6,7},{7,8},{8,9},{9,10},{10,1... | collective-permute-start | bytes 2949128 | tf_op jit(solution)/shard_map/ppermute | solution.py:15
  603.4 2.2 copy-start.4
  605.6 1.2 copy-start.3
  605.6 1.2 copy-start.7
  624.3 18.1 %copy-start.5 = (bf16[1,3,192,20,128]{4,2,1,3,0:T(8,128)(2,1)S(1)}, bf16[1,3,192,20,128]{4,2,1,3,0:T(8,128)(2,1)}, u32[]{:S(2)}) copy-start(bf16[1,3,192,20,128]{4,2,1,3,0:T(8,128)(2,1)} %copy.14) | copy-start | bytes 8847364
  636.1 7.1 %copy-start = (f32[20,192,576]{2,1,0:T(8,128)S(1)}, f32[20,192,576]{2,1,0:T(8,128)}, u32[]{:S(2)}) copy-start(f32[20,192,576]{2,1,0:T(8,128)} %copy.19) | copy-start | bytes 26542084
  643.2 3.8 copy-start.9
